TPU v7x, 32 devices: a whole 2x2x4 slice. The times are simulated.
32 devices in a mesh: outer: 8 (over y, x, core), inner: 4 (over z).
Axes of the slice: x: 2, y: 2, z: 4, core: 2. Of those that a mesh axis runs over, the one named last changes fastest.
Arguments:
- query_image: bfloat16 [2048, 1024], P(('outer', 'inner')), may hold values from -6 to 6
- key_image: bfloat16 [2048, 1024], P(('outer', 'inner')), may hold values from -6 to 6
- value_image: bfloat16 [2048, 1024], P(('outer', 'inner')), may hold values from -6 to 6
- attended_image: bfloat16 [2048, 1024], P(('outer', 'inner')), may hold values from -6 to 6
- upstream_image: bfloat16 [2048, 1024], P(('outer', 'inner')), may hold values from -128 to 128
- logsum_image: float32 [2048, 8], P(('outer', 'inner')), may hold values from 8.6 to 9.4
- query_text: bfloat16 [512, 1024], P(None, 'outer'), may hold values from -6 to 6
- key_text: bfloat16 [512, 1024], P(None, 'outer'), may hold values from -6 to 6
- value_text: bfloat16 [512, 1024], P(None, 'outer'), may hold values from -6 to 6
- attended_text: bfloat16 [512, 1024], P(None, 'outer'), may hold values from -6 to 6
- upstream_text: bfloat16 [512, 1024], P(None, 'outer'), may hold values from -128 to 128
- logsum_text: float32 [512, 8], P(None, 'outer'), may hold values from 8.6 to 9.4
Outputs:
- grad_query_image: bfloat16 [2048, 1024], P(('outer', 'inner'))
- grad_key_image: bfloat16 [2048, 1024], P(('outer', 'inner'))
- grad_value_image: bfloat16 [2048, 1024], P(('outer', 'inner'))
- grad_query_text: bfloat16 [512, 1024], P('inner', 'outer')
- grad_key_text: bfloat16 [512, 1024], P('inner', 'outer')
- grad_value_text: bfloat16 [512, 1024], P('inner', 'outer')
All inputs are finite; a program needn't handle non-finite values.
Results may differ from a plain program's by a relative error of at most 0.0055.
Values may be sent and summed in bfloat16 or wider, within the bound.
A program may use at most 64 MiB of HBM per device.

v0:
```python
import math
import jax
import jax.numpy as jnp
from jax import lax
from jax.sharding import PartitionSpec as P

HEAD_DIM = 128


def across_rows(left, right):
    return lax.dot_general(
        left, right, (((1,), (1,)), ((), ())), preferred_element_type=jnp.float32
    )


def down_rows(left, right):
    return lax.dot_general(
        left, right, (((0,), (0,)), ((), ())), preferred_element_type=jnp.float32
    )


def weights_and_mixed(queries, upstream, log_sums, deltas, keys, values):
    scores = across_rows(queries, keys) * HEAD_DIM ** (-0.5)
    weights = jnp.exp(scores - log_sums)
    slopes = across_rows(upstream, values)
    mixed = weights * (slopes - deltas)
    return (weights.astype(jnp.bfloat16), mixed.astype(jnp.bfloat16))


def query_side(mixed_half, keys):
    return jnp.dot(mixed_half, keys, preferred_element_type=jnp.float32) * HEAD_DIM ** (-0.5)


def key_side(weights_half, mixed_half, queries, upstream):
    grad_values = down_rows(weights_half, upstream)
    grad_keys = down_rows(mixed_half, queries) * HEAD_DIM ** (-0.5)
    return (grad_keys, grad_values)


def shards(
    query_image,
    key_image,
    value_image,
    attended_image,
    upstream_image,
    logsum_image,
    query_text,
    key_text,
    value_text,
    attended_text,
    upstream_text,
    logsum_text,
):
    queries, keys, values, upstream, attended = (
        lax.all_to_all(query_image, "outer", split_axis=1, concat_axis=0, tiled=True),
        lax.all_to_all(key_image, "outer", split_axis=1, concat_axis=0, tiled=True),
        lax.all_to_all(value_image, "outer", split_axis=1, concat_axis=0, tiled=True),
        lax.all_to_all(upstream_image, "outer", split_axis=1, concat_axis=0, tiled=True),
        lax.all_to_all(attended_image, "outer", split_axis=1, concat_axis=0, tiled=True),
    )
    log_sums = lax.all_to_all(logsum_image, "outer", split_axis=1, concat_axis=0, tiled=True)
    deltas = jnp.sum(
        upstream.astype(jnp.float32) * attended.astype(jnp.float32), axis=1, keepdims=True
    )
    text_deltas = jnp.sum(
        upstream_text.astype(jnp.float32) * attended_text.astype(jnp.float32), axis=1, keepdims=True
    )
    weights_half, mixed_half = weights_and_mixed(
        queries, upstream, log_sums, deltas, key_text, value_text
    )
    grad_query_near = query_side(mixed_half, key_text)
    text_key_first, text_value_first = key_side(weights_half, mixed_half, queries, upstream)
    weights_half, mixed_half = weights_and_mixed(
        query_text, upstream_text, logsum_text, text_deltas, keys, values
    )
    text_query_first = query_side(mixed_half, keys)
    grad_key_near, grad_value_near = key_side(weights_half, mixed_half, query_text, upstream_text)
    share = query_text.shape[0] // lax.axis_size("inner")
    first_row = lax.axis_index("inner") * share

    def text_rows(matrix):
        return lax.dynamic_slice_in_dim(matrix, first_row, share, 0)

    own_queries = text_rows(query_text)
    own_upstream = text_rows(upstream_text)
    weights_half, mixed_half = weights_and_mixed(
        own_queries,
        own_upstream,
        text_rows(logsum_text),
        text_rows(text_deltas),
        key_text,
        value_text,
    )
    text_query_rows = query_side(mixed_half, key_text)
    text_key_second, text_value_second = key_side(
        weights_half, mixed_half, own_queries, own_upstream
    )
    text_query = lax.dynamic_update_slice_in_dim(
        text_query_first, text_rows(text_query_first) + text_query_rows, first_row, 0
    )
    zero_rows = jnp.zeros(queries.shape, jnp.float32)
    whole_keys, whole_values = (
        lax.all_gather(keys, "inner", axis=0, tiled=True),
        lax.all_gather(values, "inner", axis=0, tiled=True),
    )
    key_count = whole_keys.shape[0]
    size = math.gcd(key_count, 1024)
    count = key_count // size
    stacked_keys = whole_keys.reshape(count, size, whole_keys.shape[1])
    stacked_values = whole_values.reshape(count, size, whole_values.shape[1])

    def key_block(carry, block):
        weights_block, mixed_block = weights_and_mixed(
            queries, upstream, log_sums, deltas, block[0], block[1]
        )
        terms = key_side(weights_block, mixed_block, queries, upstream)
        return (carry + query_side(mixed_block, block[0]), terms)

    grad_query_far, stacked_terms = lax.scan(key_block, zero_rows, (stacked_keys, stacked_values))
    key_terms = stacked_terms[0].reshape(key_count, whole_keys.shape[1])
    value_terms = stacked_terms[1].reshape(key_count, whole_keys.shape[1])
    grad_key_far, grad_value_far = (
        lax.psum_scatter(key_terms, "inner", scatter_dimension=0, tiled=True),
        lax.psum_scatter(value_terms, "inner", scatter_dimension=0, tiled=True),
    )
    head_grads = (
        (grad_query_near + grad_query_far).astype(jnp.bfloat16),
        (grad_key_near + grad_key_far).astype(jnp.bfloat16),
        (grad_value_near + grad_value_far).astype(jnp.bfloat16),
    )
    image_query, image_key, image_value = (
        lax.all_to_all(head_grads[0], "outer", split_axis=0, concat_axis=1, tiled=True),
        lax.all_to_all(head_grads[1], "outer", split_axis=0, concat_axis=1, tiled=True),
        lax.all_to_all(head_grads[2], "outer", split_axis=0, concat_axis=1, tiled=True),
    )
    summed_query, summed_key, summed_value = (
        lax.psum_scatter(text_query, "inner", scatter_dimension=0, tiled=True),
        lax.psum_scatter(
            text_key_first + text_key_second, "inner", scatter_dimension=0, tiled=True
        ),
        lax.psum_scatter(
            text_value_first + text_value_second, "inner", scatter_dimension=0, tiled=True
        ),
    )
    return (
        image_query,
        image_key,
        image_value,
        summed_query.astype(jnp.bfloat16),
        summed_key.astype(jnp.bfloat16),
        summed_value.astype(jnp.bfloat16),
    )


def solution(mesh):
    in_specs = (
        P(("outer", "inner"), None),
        P(("outer", "inner"), None),
        P(("outer", "inner"), None),
        P(("outer", "inner"), None),
        P(("outer", "inner"), None),
        P(("outer", "inner"), None),
        P(None, "outer"),
        P(None, "outer"),
        P(None, "outer"),
        P(None, "outer"),
        P(None, "outer"),
        P(None, "outer"),
    )
    out_specs = (
        P(("outer", "inner"), None),
        P(("outer", "inner"), None),
        P(("outer", "inner"), None),
        P("inner", "outer"),
        P("inner", "outer"),
        P("inner", "outer"),
    )
    return jax.shard_map(shards, mesh=mesh, in_specs=in_specs, out_specs=out_specs, check_vma=False)
```

profile of v0, /device:TPU:0, one launch (start us, length us, event | category | flops | bytes accessed | tf_op | source)
XLA Modules:
  0.0 203.6 jit_solution(8097618321480912621)
XLA Ops:
  7.2 5.3 %all-to-all-start.1 = ((f32[64,8,1]{0,2,1:T(1,128)}), f32[64,8,1]{0,2,1:T(1,128)S(1)}, u32[]{:S(2)}, u32[]{:S(2)}) async-start(f32[64,8,1]{0,2,1:T(1,128)} %bitcast.168), calls=%async_computation.1 | async-start | bytes 8192 | tf_op jit(solution)/shard_map/all_to_all | solution.py:61
  22.0 4.2 %all-to-all-start.4 = ((bf16[64,8,128]{2,0,1:T(8,128)(2,1)}), bf16[64,8,128]{2,0,1:T(8,128)(2,1)S(1)}, u32[]{:S(2)}, u32[]{:S(2)}) async-start(bf16[64,8,128]{2,0,1:T(8,128)(2,1)} %copy_bitcast_fusion.4), calls=%async_computation.4 | async-start | bytes 262144 | tf_op jit(solution)/shard_map/all_to_all | solution.py:56
  27.1 4.6 %all-to-all-done.4 = bf16[64,8,128]{2,0,1:T(8,128)(2,1)S(1)} async-done(((bf16[64,8,128]{2,0,1:T(8,128)(2,1)}), bf16[64,8,128]{2,0,1:T(8,128)(2,1)S(1)}, u32[]{:S(2)}, u32[]{:S(2)}) %all-to-all-start.4) | async-done | bytes 131104 | tf_op jit(solution)/shard_map/all_to_all | solution.py:56
  31.7 3.4 %all-to-all-start.5 = ((bf16[64,8,128]{2,0,1:T(8,128)(2,1)}), bf16[64,8,128]{2,0,1:T(8,128)(2,1)S(1)}, u32[]{:S(2)}, u32[]{:S(2)}) async-start(bf16[64,8,128]{2,0,1:T(8,128)(2,1)} %copy_bitcast_fusion.3), calls=%async_computation.5 | async-start | bytes 262144 | tf_op jit(solution)/shard_map/all_to_all | solution.py:57
  35.4 5.1 %all-to-all-done.5 = bf16[64,8,128]{2,0,1:T(8,128)(2,1)S(1)} async-done(((bf16[64,8,128]{2,0,1:T(8,128)(2,1)}), bf16[64,8,128]{2,0,1:T(8,128)(2,1)S(1)}, u32[]{:S(2)}, u32[]{:S(2)}) %all-to-all-start.5) | async-done | bytes 131104 | tf_op jit(solution)/shard_map/all_to_all | solution.py:57
  40.5 3.4 %all-to-all-start.2 = ((bf16[64,8,128]{2,0,1:T(8,128)(2,1)}), bf16[64,8,128]{2,0,1:T(8,128)(2,1)S(1)}, u32[]{:S(2)}, u32[]{:S(2)}) async-start(bf16[64,8,128]{2,0,1:T(8,128)(2,1)} %copy_bitcast_fusion.6), calls=%async_computation.2 | async-start | bytes 262144 | tf_op jit(solution)/shard_map/all_to_all | solution.py:58
  45.3 4.0 %all-to-all-done.2 = bf16[64,8,128]{2,0,1:T(8,128)(2,1)S(1)} async-done(((bf16[64,8,128]{2,0,1:T(8,128)(2,1)}), bf16[64,8,128]{2,0,1:T(8,128)(2,1)S(1)}, u32[]{:S(2)}, u32[]{:S(2)}) %all-to-all-start.2) | async-done | bytes 131104 | tf_op jit(solution)/shard_map/all_to_all | solution.py:58
  49.3 3.4 %all-to-all-start.3 = ((bf16[64,8,128]{2,0,1:T(8,128)(2,1)}), bf16[64,8,128]{2,0,1:T(8,128)(2,1)S(1)}, u32[]{:S(2)}, u32[]{:S(2)}) async-start(bf16[64,8,128]{2,0,1:T(8,128)(2,1)} %copy_bitcast_fusion.5), calls=%async_computation.3 | async-start | bytes 262144 | tf_op jit(solution)/shard_map/all_to_all | solution.py:59
  52.9 5.2 %all-to-all-done.3 = bf16[64,8,128]{2,0,1:T(8,128)(2,1)S(1)} async-done(((bf16[64,8,128]{2,0,1:T(8,128)(2,1)}), bf16[64,8,128]{2,0,1:T(8,128)(2,1)S(1)}, u32[]{:S(2)}, u32[]{:S(2)}) %all-to-all-start.3) | async-done | bytes 131104 | tf_op jit(solution)/shard_map/all_to_all | solution.py:59
  58.1 3.4 %all-to-all-start = ((bf16[64,8,128]{2,0,1:T(8,128)(2,1)}), bf16[64,8,128]{2,0,1:T(8,128)(2,1)S(1)}, u32[]{:S(2)}, u32[]{:S(2)}) async-start(bf16[64,8,128]{2,0,1:T(8,128)(2,1)} %copy_bitcast_fusion.7), calls=%async_computation | async-start | bytes 262144 | tf_op jit(solution)/shard_map/all_to_all | solution.py:55
  62.3 4.6 %all-to-all-done = bf16[64,8,128]{2,0,1:T(8,128)(2,1)S(1)} async-done(((bf16[64,8,128]{2,0,1:T(8,128)(2,1)}), bf16[64,8,128]{2,0,1:T(8,128)(2,1)S(1)}, u32[]{:S(2)}, u32[]{:S(2)}) %all-to-all-start) | async-done | bytes 131104 | tf_op jit(solution)/shard_map/all_to_all | solution.py:55
  67.6 19.9 %all_gather.6 = bf16[2048,128]{1,0:T(8,128)(2,1)S(1)} all-gather(bf16[512,128]{1,0:T(8,128)(2,1)S(1)} %bitcast.158), channel_id=1, replica_groups=mesh['outer'=8,'inner'=4] {'inner'}, dimensions={0}, use_global_device_ids=true | all-gather | bytes 655360 | tf_op jit(solution)/shard_map/all_gather | solution.py:103
  88.9 17.1 %all_gather.7 = bf16[2048,128]{1,0:T(8,128)(2,1)} all-gather(bf16[512,128]{1,0:T(8,128)(2,1)S(1)} %bitcast.160), channel_id=1, replica_groups=mesh['outer'=8,'inner'=4] {'inner'}, dimensions={0}, use_global_device_ids=true | all-gather | bytes 655360 | tf_op jit(solution)/shard_map/all_gather | solution.py:104
  107.4 13.6 %while.15 = (s32[]{:T(128)}, f32[512,128]{1,0:T(8,128)}, f32[2,1024,128]{2,1,0:T(8,128)}, f32[2,1024,128]{2,1,0:T(8,128)}, bf16[2,1024,128]{2,1,0:T(8,128)(2,1)S...) while((s32[]{:T(128)}, f32[512,128]{1,0:T(8,128)}, ...), condition=%wide.region_2.3_spmd.clone, body=%wide.region_1.0_spmd.clone.sunk | while | flops 675610624 | bytes 27007272 | solution.py:119
  109.2 2.2 %fusion.116 = f32[512,128]{1,0:T(8,128)} fusion(bf16[1024,512]{1,0:T(8,128)(2,1)S(1)} %multiply_convert_fusion.2, f32[512,128]{1,0:T(8,128)} %get-tuple-element.190, bf16[2,1024,128]{2,1,0:T(8,128)(2,1)} %copy-done.1, s32[]{:T(128)S(6)} %copy.62, pred[]{:T(512)S(6)} %compare.3), kind=kOutput, calls=%fused_computation.9.clone.1 | convolution fusion | flops 134414336 | bytes 1835013 | tf_op jit(solution)/shard_map/while/body/eval_jaxpr/dot_general | solution.py:31
  116.0 2.3 %fusion.116 = f32[512,128]{1,0:T(8,128)} fusion(bf16[1024,512]{1,0:T(8,128)(2,1)S(1)} %multiply_convert_fusion.2, f32[512,128]{1,0:T(8,128)} %get-tuple-element.190, bf16[2,1024,128]{2,1,0:T(8,128)(2,1)} %copy-done.1, s32[]{:T(128)S(6)} %copy.62, pred[]{:T(512)S(6)} %compare.3), kind=kOutput, calls=%fused_computation.9.clone.1 | convolution fusion | flops 134414336 | bytes 1835013 | tf_op jit(solution)/shard_map/while/body/eval_jaxpr/dot_general | solution.py:31
  122.4 7.9 %all_to_all.165 = bf16[8,64,128]{2,1,0:T(8,128)(2,1)S(1)} all-to-all(bf16[8,64,128]{2,1,0:T(8,128)(2,1)S(1)} %bitcast.163), channel_id=1, replica_groups=mesh['outer'=8,'inner'=4] {'outer'}, dimensions={0} | all-to-all | bytes 262144 | tf_op jit(solution)/shard_map/all_to_all | solution.py:132
  135.3 22.0 %reduce-scatter.6.cloned.1.call-done = f32[512,128]{1,0:T(8,128)} async-done(((f32[2048,128]{1,0:T(8,128)}), f32[512,128]{1,0:T(8,128)}) %reduce-scatter.6.cloned.1.call-update) | async-done | bytes 262160 | tf_op jit(solution)/shard_map/reduce_scatter | solution.py:123
  157.3 2.0 fusion.35
  159.3 3.6 %all-to-all-start.7 = ((bf16[8,64,128]{2,1,0:T(8,128)(2,1)}), bf16[8,64,128]{2,1,0:T(8,128)(2,1)S(1)}, u32[]{:S(2)}, u32[]{:S(2)}) async-start(bf16[8,64,128]{2,1,0:T(8,128)(2,1)} %bitcast.21), calls=%async_computation.8 | async-start | bytes 262144 | tf_op jit(solution)/shard_map/all_to_all | solution.py:133
  162.9 22.3 %reduce-scatter.8.cloned.1.call-done = f32[512,128]{1,0:T(8,128)} async-done(((f32[2048,128]{1,0:T(8,128)}), f32[512,128]{1,0:T(8,128)}) %reduce-scatter.8.cloned.1.call-update) | async-done | bytes 262160 | tf_op jit(solution)/shard_map/reduce_scatter | solution.py:124
  185.3 2.0 fusion.33
  187.2 3.6 %all-to-all-start.8 = ((bf16[8,64,128]{2,1,0:T(8,128)(2,1)}), bf16[8,64,128]{2,1,0:T(8,128)(2,1)S(1)}, u32[]{:S(2)}, u32[]{:S(2)}) async-start(bf16[8,64,128]{2,1,0:T(8,128)(2,1)} %bitcast.24), calls=%async_computation.10 | async-start | bytes 262144 | tf_op jit(solution)/shard_map/all_to_all | solution.py:134
  191.5 4.8 %all-to-all-done.8 = bf16[8,64,128]{2,1,0:T(8,128)(2,1)S(1)} async-done(((bf16[8,64,128]{2,1,0:T(8,128)(2,1)}), bf16[8,64,128]{2,1,0:T(8,128)(2,1)S(1)}, u32[]{:S(2)}, u32[]{:S(2)}) %all-to-all-start.8) | async-done | bytes 131104 | tf_op jit(solution)/shard_map/all_to_all | solution.py:134
  (113 shorter events, 33.1 us)
Async XLA Ops:
  7.2 27.9 %copy-start.21 = (f32[512,1]{0,1:T(1,128)S(1)}, f32[512,1]{0,1:T(1,128)}, u32[]{:S(2)}) copy-start(f32[512,1]{0,1:T(1,128)} %param.25) | copy-start | bytes 6148
  7.2 27.9 %copy-start.16 = (bf16[512,128]{1,0:T(8,128)(2,1)S(1)}, bf16[512,128]{1,0:T(8,128)(2,1)}, u32[]{:S(2)}) copy-start(bf16[512,128]{1,0:T(8,128)(2,1)} %param.20) | copy-start | bytes 393220
  7.2 19.0 %copy-start.20 = (bf16[64,1024]{1,0:T(8,128)(2,1)S(1)}, bf16[64,1024]{1,0:T(8,128)(2,1)}, u32[]{:S(2)}) copy-start(bf16[64,1024]{1,0:T(8,128)(2,1)} %param.17) | copy-start | bytes 393220
  7.2 14.8 %all-to-all-start.1 = ((f32[64,8,1]{0,2,1:T(1,128)}), f32[64,8,1]{0,2,1:T(1,128)S(1)}, u32[]{:S(2)}, u32[]{:S(2)}) async-start(f32[64,8,1]{0,2,1:T(1,128)} %bitcast.168), calls=%async_computation.1 | async-start | bytes 8192 | tf_op jit(solution)/shard_map/all_to_all | solution.py:61
  15.7 28.2 %copy-start.11 = (bf16[512,128]{1,0:T(8,128)(2,1)S(1)}, bf16[512,128]{1,0:T(8,128)(2,1)}, u32[]{:S(2)}) copy-start(bf16[512,128]{1,0:T(8,128)(2,1)} %param.24) | copy-start | bytes 393220
  22.0 9.7 %all-to-all-start.4 = ((bf16[64,8,128]{2,0,1:T(8,128)(2,1)}), bf16[64,8,128]{2,0,1:T(8,128)(2,1)S(1)}, u32[]{:S(2)}, u32[]{:S(2)}) async-start(bf16[64,8,128]{2,0,1:T(8,128)(2,1)} %copy_bitcast_fusion.4), calls=%async_computation.4 | async-start | bytes 262144 | tf_op jit(solution)/shard_map/all_to_all | solution.py:56
  31.7 8.8 %all-to-all-start.5 = ((bf16[64,8,128]{2,0,1:T(8,128)(2,1)}), bf16[64,8,128]{2,0,1:T(8,128)(2,1)S(1)}, u32[]{:S(2)}, u32[]{:S(2)}) async-start(bf16[64,8,128]{2,0,1:T(8,128)(2,1)} %copy_bitcast_fusion.3), calls=%async_computation.5 | async-start | bytes 262144 | tf_op jit(solution)/shard_map/all_to_all | solution.py:57
  35.4 22.7 %copy-start.4 = (f32[512,512]{1,0:T(8,128)}, f32[512,512]{1,0:T(8,128)S(1)}, u32[]{:S(2)}) copy-start(f32[512,512]{1,0:T(8,128)S(1)} %fusion.23) | copy-start | bytes 3145732
  40.5 8.8 %all-to-all-start.2 = ((bf16[64,8,128]{2,0,1:T(8,128)(2,1)}), bf16[64,8,128]{2,0,1:T(8,128)(2,1)S(1)}, u32[]{:S(2)}, u32[]{:S(2)}) async-start(bf16[64,8,128]{2,0,1:T(8,128)(2,1)} %copy_bitcast_fusion.6), calls=%async_computation.2 | async-start | bytes 262144 | tf_op jit(solution)/shard_map/all_to_all | solution.py:58
  45.0 22.3 %copy-start.18 = (bf16[512,128]{1,0:T(8,128)(2,1)S(1)}, bf16[512,128]{1,0:T(8,128)(2,1)}, u32[]{:S(2)}) copy-start(bf16[512,128]{1,0:T(8,128)(2,1)} %param.22) | copy-start | bytes 393220
  49.3 8.8 %all-to-all-start.3 = ((bf16[64,8,128]{2,0,1:T(8,128)(2,1)}), bf16[64,8,128]{2,0,1:T(8,128)(2,1)S(1)}, u32[]{:S(2)}, u32[]{:S(2)}) async-start(bf16[64,8,128]{2,0,1:T(8,128)(2,1)} %copy_bitcast_fusion.5), calls=%async_computation.3 | async-start | bytes 262144 | tf_op jit(solution)/shard_map/all_to_all | solution.py:59
  58.1 8.8 %all-to-all-start = ((bf16[64,8,128]{2,0,1:T(8,128)(2,1)}), bf16[64,8,128]{2,0,1:T(8,128)(2,1)S(1)}, u32[]{:S(2)}, u32[]{:S(2)}) async-start(bf16[64,8,128]{2,0,1:T(8,128)(2,1)} %copy_bitcast_fusion.7), calls=%async_computation | async-start | bytes 262144 | tf_op jit(solution)/shard_map/all_to_all | solution.py:55
  61.5 69.4 %reduce-scatter.10.cloned.1.call-start = ((), (), s32[]{:S(2)}) async-start(), calls=%async_computation.16 | async-start | bytes 327680 | tf_op jit(solution)/shard_map/reduce_scatter | solution.py:137
  62.3 70.2 %reduce-scatter.12.cloned.1.call-start = ((), (), s32[]{:S(2)}) async-start(), calls=%async_computation.17 | async-start | bytes 327680 | tf_op jit(solution)/shard_map/reduce_scatter | solution.py:138
  67.6 38.7 %copy-start.9 = (bf16[512,512]{1,0:T(8,128)(2,1)}, bf16[512,512]{1,0:T(8,128)(2,1)S(1)}, u32[]{:S(2)}) copy-start(bf16[512,512]{1,0:T(8,128)(2,1)S(1)} %fusion.26) | copy-start | bytes 1572868
  88.8 45.0 %reduce-scatter.14.cloned.1.call-start = ((), (), s32[]{:S(2)}) async-start(), calls=%async_computation.18 | async-start | bytes 327680 | tf_op jit(solution)/shard_map/reduce_scatter | solution.py:141
  107.3 50.0 %reduce-scatter.6.cloned.1.call-start = ((), (), s32[]{:S(2)}) async-start(), calls=%async_computation.14 | async-start | bytes 1310720 | tf_op jit(solution)/shard_map/reduce_scatter | solution.py:123
  121.0 36.4 %copy-start.8 = (bf16[512,512]{1,0:T(8,128)(2,1)S(1)}, bf16[512,512]{1,0:T(8,128)(2,1)}, u32[]{:S(2)}) copy-start(bf16[512,512]{1,0:T(8,128)(2,1)} %copy-done.7) | copy-start | bytes 1572868
  121.0 36.4 %copy-start.17 = (bf16[512,128]{1,0:T(8,128)(2,1)S(1)}, bf16[512,128]{1,0:T(8,128)(2,1)}, u32[]{:S(2)}) copy-start(bf16[512,128]{1,0:T(8,128)(2,1)} %param.20) | copy-start | bytes 393220
  121.0 64.3 %reduce-scatter.8.cloned.1.call-start = ((), (), s32[]{:S(2)}) async-start(), calls=%async_computation.15 | async-start | bytes 1310720 | tf_op jit(solution)/shard_map/reduce_scatter | solution.py:124
  121.1 64.2 %copy-start.5 = (f32[512,512]{1,0:T(8,128)S(1)}, f32[512,512]{1,0:T(8,128)}, u32[]{:S(2)}) copy-start(f32[512,512]{1,0:T(8,128)} %copy-done.4) | copy-start | bytes 3145732
  121.1 64.2 %copy-start.12 = (bf16[512,128]{1,0:T(8,128)(2,1)S(1)}, bf16[512,128]{1,0:T(8,128)(2,1)}, u32[]{:S(2)}) copy-start(bf16[512,128]{1,0:T(8,128)(2,1)} %param.24) | copy-start | bytes 393220
  159.3 27.9 %all-to-all-start.7 = ((bf16[8,64,128]{2,1,0:T(8,128)(2,1)}), bf16[8,64,128]{2,1,0:T(8,128)(2,1)S(1)}, u32[]{:S(2)}, u32[]{:S(2)}) async-start(bf16[8,64,128]{2,1,0:T(8,128)(2,1)} %bitcast.21), calls=%async_computation.8 | async-start | bytes 262144 | tf_op jit(solution)/shard_map/all_to_all | solution.py:133
  187.2 9.1 %all-to-all-start.8 = ((bf16[8,64,128]{2,1,0:T(8,128)(2,1)}), bf16[8,64,128]{2,1,0:T(8,128)(2,1)S(1)}, u32[]{:S(2)}, u32[]{:S(2)}) async-start(bf16[8,64,128]{2,1,0:T(8,128)(2,1)} %bitcast.24), calls=%async_computation.10 | async-start | bytes 262144 | tf_op jit(solution)/shard_map/all_to_all | solution.py:134
  (16 other events, 54.0 us)
Sparse Core Ops, SparseCore 0:
  64.6 23.0 reduce-scatter.9
  89.9 19.1 reduce-scatter.11
  111.4 18.1 reduce-scatter.13
  131.8 25.5 reduce-scatter.5
  159.5 25.7 reduce-scatter.7
where the time goes:
time: 205 us; the launch traced here: 204 us
  waiting for transfers between devices  73.8 us (36%)
  blocking collectives  44.9 us (22%)
  starting transfers between devices  30.5 us (15%)
  matrix products  20.5 us (10%)
  local copies, waits for them, and re-layouts  14.2 us (7%)
  between operations  14.1 us (7%)
  other arithmetic  5.63 us (3%)
    reduce_scatter x1, waiting for transfers between devices, shards(): lax.psum_scatter(value_terms, 'inner', scatter_dimension=0, tiled=True)  22.3 us
    reduce_scatter x1, waiting for transfers between devices, shards(): lax.psum_scatter(key_terms, 'inner', scatter_dimension=0, tiled=True)  22 us
    all_gather x1, blocking collectives, shards(): lax.all_gather(keys, 'inner', axis=0, tiled=True)  19.9 us
    all_gather x1, blocking collectives, shards(): lax.all_gather(values, 'inner', axis=0, tiled=True)  17.1 us
    dot_general x10, matrix products, down_rows(): lax.dot_general(left, right, (((0,), (0,)), ((), ())), preferred_element_...  9.88 us
    all_to_all x1, blocking collectives, shards(): lax.all_to_all(head_grads[0], 'outer', split_axis=0, concat_axis=1, tiled...  7.89 us
    all_to_all x1, starting transfers between devices, shards(): lax.all_to_all(logsum_image, 'outer', split_axis=1, concat_axis=0, tiled=...  5.34 us
    dot_general x10, matrix products, across_rows(): lax.dot_general(left, right, (((1,), (1,)), ((), ())), preferred_element_...  5.31 us
  transfers between devices with their start and end apart: 13, of which 8 were waited for; matrix products, arithmetic and copies ran while one was open for 17% of the time, Pallas kernels for 0%

commit v1 on v0

--- a/solution.py
+++ b/solution.py
@@ -5,6 +5,13 @@
 from jax.sharding import PartitionSpec as P
 
 HEAD_DIM = 128
+
+
+def match_cycles(slab_in, ax_name):
+    local_next = lax.axis_size(ax_name)
+    new = jnp.split(slab_in, local_next, axis=1)
+    t_next = jnp.stack(new, axis=0)
+    return jnp.concatenate(lax.all_to_all(t_next, ax_name, 0, 0), axis=0)
 
 
 def across_rows(left, right):
@@ -53,7 +60,7 @@
 ):
     queries, keys, values, upstream, attended = (
         lax.all_to_all(query_image, "outer", split_axis=1, concat_axis=0, tiled=True),
-        lax.all_to_all(key_image, "outer", split_axis=1, concat_axis=0, tiled=True),
+        match_cycles(key_image, "outer"),
         lax.all_to_all(value_image, "outer", split_axis=1, concat_axis=0, tiled=True),
         lax.all_to_all(upstream_image, "outer", split_axis=1, concat_axis=0, tiled=True),
         lax.all_to_all(attended_image, "outer", split_axis=1, concat_axis=0, tiled=True),

time: 205 us -> 215 us (1.049)
  local copies, waits for them, and re-layouts: 14.2 us -> 24 us
    unnamed x34 -> x39, local copies, waits for them, and re-layouts: 1.37 us -> 10.6 us
  transfers between devices with their start and end apart: 13 -> 13, of which waited for: 8 -> 8; matrix products, arithmetic and copies ran while one was open for 17% -> 21% of each run, Pallas kernels for 0% -> 0%
where the time goes in v1:
time: 215 us; the launch traced here: 213 us
  waiting for transfers between devices  73.8 us (34%)
  blocking collectives  44.9 us (21%)
  starting transfers between devices  30.6 us (14%)
  local copies, waits for them, and re-layouts  24 us (11%)
  matrix products  20.4 us (9%)
  between operations  14.1 us (7%)
  other arithmetic  5.63 us (3%)
    reduce_scatter x1, waiting for transfers between devices, shards(): lax.psum_scatter(value_terms, 'inner', scatter_dimension=0, tiled=True)  22.4 us
    reduce_scatter x1, waiting for transfers between devices, shards(): lax.psum_scatter(key_terms, 'inner', scatter_dimension=0, tiled=True)  22 us
    all_gather x1, blocking collectives, shards(): lax.all_gather(keys, 'inner', axis=0, tiled=True)  19.9 us
    all_gather x1, blocking collectives, shards(): lax.all_gather(values, 'inner', axis=0, tiled=True)  17.1 us
    unnamed x39, local copies, waits for them, and re-layouts  10.6 us
    dot_general x10, matrix products, down_rows(): lax.dot_general(left, right, (((0,), (0,)), ((), ())), preferred_element_...  9.74 us
    all_to_all x1, blocking collectives, shards(): lax.all_to_all(head_grads[0], 'outer', split_axis=0, concat_axis=1, tiled...  7.89 us
    all_to_all x1, starting transfers between devices, shards(): lax.all_to_all(logsum_image, 'outer', split_axis=1, concat_axis=0, tiled=...  5.34 us
  transfers between devices with their start and end apart: 13, of which 8 were waited for; matrix products, arithmetic and copies ran while one was open for 21% of the time, Pallas kernels for 0%

profile of v1, /device:TPU:0, one launch (start us, length us, event | category | flops | bytes accessed | tf_op | source)
XLA Modules:
  0.0 213.4 jit_solution(17294467540245437668)
XLA Ops:
  7.2 5.3 %all-to-all-start.1 = ((f32[64,8,1]{0,2,1:T(1,128)}), f32[64,8,1]{0,2,1:T(1,128)S(1)}, u32[]{:S(2)}, u32[]{:S(2)}) async-start(f32[64,8,1]{0,2,1:T(1,128)} %bitcast.179), calls=%async_computation.1 | async-start | bytes 8192 | tf_op jit(solution)/shard_map/all_to_all | solution.py:68
  31.9 4.2 %all-to-all-start.4 = ((bf16[8,64,128]{2,1,0:T(8,128)(2,1)}), bf16[8,64,128]{2,1,0:T(8,128)(2,1)S(1)}, u32[]{:S(2)}, u32[]{:S(2)}) async-start(bf16[8,64,128]{2,1,0:T(8,128)(2,1)} %constant_dynamic-update-slice_fusion), calls=%async_computation.4 | async-start | bytes 262144 | tf_op jit(solution)/shard_map/all_to_all | solution.py:14
  36.9 4.6 %all-to-all-done.4 = bf16[8,64,128]{2,1,0:T(8,128)(2,1)S(1)} async-done(((bf16[8,64,128]{2,1,0:T(8,128)(2,1)}), bf16[8,64,128]{2,1,0:T(8,128)(2,1)S(1)}, u32[]{:S(2)}, u32[]{:S(2)}) %all-to-all-start.4) | async-done | bytes 131104 | tf_op jit(solution)/shard_map/all_to_all | solution.py:14
  41.6 3.4 %all-to-all-start.5 = ((bf16[64,8,128]{2,0,1:T(8,128)(2,1)}), bf16[64,8,128]{2,0,1:T(8,128)(2,1)S(1)}, u32[]{:S(2)}, u32[]{:S(2)}) async-start(bf16[64,8,128]{2,0,1:T(8,128)(2,1)} %copy_bitcast_fusion.3), calls=%async_computation.5 | async-start | bytes 262144 | tf_op jit(solution)/shard_map/all_to_all | solution.py:64
  45.3 5.1 %all-to-all-done.5 = bf16[64,8,128]{2,0,1:T(8,128)(2,1)S(1)} async-done(((bf16[64,8,128]{2,0,1:T(8,128)(2,1)}), bf16[64,8,128]{2,0,1:T(8,128)(2,1)S(1)}, u32[]{:S(2)}, u32[]{:S(2)}) %all-to-all-start.5) | async-done | bytes 131104 | tf_op jit(solution)/shard_map/all_to_all | solution.py:64
  50.4 3.4 %all-to-all-start.2 = ((bf16[64,8,128]{2,0,1:T(8,128)(2,1)}), bf16[64,8,128]{2,0,1:T(8,128)(2,1)S(1)}, u32[]{:S(2)}, u32[]{:S(2)}) async-start(bf16[64,8,128]{2,0,1:T(8,128)(2,1)} %copy_bitcast_fusion.5), calls=%async_computation.2 | async-start | bytes 262144 | tf_op jit(solution)/shard_map/all_to_all | solution.py:65
  55.2 4.0 %all-to-all-done.2 = bf16[64,8,128]{2,0,1:T(8,128)(2,1)S(1)} async-done(((bf16[64,8,128]{2,0,1:T(8,128)(2,1)}), bf16[64,8,128]{2,0,1:T(8,128)(2,1)S(1)}, u32[]{:S(2)}, u32[]{:S(2)}) %all-to-all-start.2) | async-done | bytes 131104 | tf_op jit(solution)/shard_map/all_to_all | solution.py:65
  59.2 3.4 %all-to-all-start.3 = ((bf16[64,8,128]{2,0,1:T(8,128)(2,1)}), bf16[64,8,128]{2,0,1:T(8,128)(2,1)S(1)}, u32[]{:S(2)}, u32[]{:S(2)}) async-start(bf16[64,8,128]{2,0,1:T(8,128)(2,1)} %copy_bitcast_fusion.4), calls=%async_computation.3 | async-start | bytes 262144 | tf_op jit(solution)/shard_map/all_to_all | solution.py:66
  62.8 5.2 %all-to-all-done.3 = bf16[64,8,128]{2,0,1:T(8,128)(2,1)S(1)} async-done(((bf16[64,8,128]{2,0,1:T(8,128)(2,1)}), bf16[64,8,128]{2,0,1:T(8,128)(2,1)S(1)}, u32[]{:S(2)}, u32[]{:S(2)}) %all-to-all-start.3) | async-done | bytes 131104 | tf_op jit(solution)/shard_map/all_to_all | solution.py:66
  68.0 3.4 %all-to-all-start = ((bf16[64,8,128]{2,0,1:T(8,128)(2,1)}), bf16[64,8,128]{2,0,1:T(8,128)(2,1)S(1)}, u32[]{:S(2)}, u32[]{:S(2)}) async-start(bf16[64,8,128]{2,0,1:T(8,128)(2,1)} %copy_bitcast_fusion.6), calls=%async_computation | async-start | bytes 262144 | tf_op jit(solution)/shard_map/all_to_all | solution.py:62
  72.2 4.6 %all-to-all-done = bf16[64,8,128]{2,0,1:T(8,128)(2,1)S(1)} async-done(((bf16[64,8,128]{2,0,1:T(8,128)(2,1)}), bf16[64,8,128]{2,0,1:T(8,128)(2,1)S(1)}, u32[]{:S(2)}, u32[]{:S(2)}) %all-to-all-start) | async-done | bytes 131104 | tf_op jit(solution)/shard_map/all_to_all | solution.py:62
  77.5 19.9 %all_gather.6 = bf16[2048,128]{1,0:T(8,128)(2,1)S(1)} all-gather(bf16[512,128]{1,0:T(8,128)(2,1)S(1)} %bitcast.169), channel_id=1, replica_groups=mesh['outer'=8,'inner'=4] {'inner'}, dimensions={0}, use_global_device_ids=true | all-gather | bytes 655360 | tf_op jit(solution)/shard_map/all_gather | solution.py:110
  98.8 17.1 %all_gather.7 = bf16[2048,128]{1,0:T(8,128)(2,1)} all-gather(bf16[512,128]{1,0:T(8,128)(2,1)S(1)} %bitcast.171), channel_id=1, replica_groups=mesh['outer'=8,'inner'=4] {'inner'}, dimensions={0}, use_global_device_ids=true | all-gather | bytes 655360 | tf_op jit(solution)/shard_map/all_gather | solution.py:111
  117.3 13.6 %while.15 = (s32[]{:T(128)}, f32[512,128]{1,0:T(8,128)}, f32[2,1024,128]{2,1,0:T(8,128)}, f32[2,1024,128]{2,1,0:T(8,128)}, bf16[2,1024,128]{2,1,0:T(8,128)(2,1)S...) while((s32[]{:T(128)}, f32[512,128]{1,0:T(8,128)}, ...), condition=%wide.region_2.3_spmd.clone, body=%wide.region_1.0_spmd.clone.sunk | while | flops 675610624 | bytes 27007272 | solution.py:126
  119.1 2.2 %fusion.116 = f32[512,128]{1,0:T(8,128)} fusion(bf16[1024,512]{1,0:T(8,128)(2,1)S(1)} %multiply_convert_fusion.2, f32[512,128]{1,0:T(8,128)} %get-tuple-element.190, bf16[2,1024,128]{2,1,0:T(8,128)(2,1)} %copy-done.1, s32[]{:T(128)S(6)} %copy.69, pred[]{:T(512)S(6)} %compare.3), kind=kOutput, calls=%fused_computation.9.clone.1 | convolution fusion | flops 134414336 | bytes 1835013 | tf_op jit(solution)/shard_map/while/body/eval_jaxpr/dot_general | solution.py:38
  125.8 2.3 %fusion.116 = f32[512,128]{1,0:T(8,128)} fusion(bf16[1024,512]{1,0:T(8,128)(2,1)S(1)} %multiply_convert_fusion.2, f32[512,128]{1,0:T(8,128)} %get-tuple-element.190, bf16[2,1024,128]{2,1,0:T(8,128)(2,1)} %copy-done.1, s32[]{:T(128)S(6)} %copy.69, pred[]{:T(512)S(6)} %compare.3), kind=kOutput, calls=%fused_computation.9.clone.1 | convolution fusion | flops 134414336 | bytes 1835013 | tf_op jit(solution)/shard_map/while/body/eval_jaxpr/dot_general | solution.py:38
  132.3 7.9 %all_to_all.151 = bf16[8,64,128]{2,1,0:T(8,128)(2,1)S(1)} all-to-all(bf16[8,64,128]{2,1,0:T(8,128)(2,1)S(1)} %bitcast.174), channel_id=1, replica_groups=mesh['outer'=8,'inner'=4] {'outer'}, dimensions={0} | all-to-all | bytes 262144 | tf_op jit(solution)/shard_map/all_to_all | solution.py:139
  145.2 22.0 %reduce-scatter.6.cloned.1.call-done = f32[512,128]{1,0:T(8,128)} async-done(((f32[2048,128]{1,0:T(8,128)}), f32[512,128]{1,0:T(8,128)}) %reduce-scatter.6.cloned.1.call-update) | async-done | bytes 262160 | tf_op jit(solution)/shard_map/reduce_scatter | solution.py:130
  167.2 1.9 fusion.36
  169.1 3.7 %all-to-all-start.7 = ((bf16[8,64,128]{2,1,0:T(8,128)(2,1)}), bf16[8,64,128]{2,1,0:T(8,128)(2,1)S(1)}, u32[]{:S(2)}, u32[]{:S(2)}) async-start(bf16[8,64,128]{2,1,0:T(8,128)(2,1)} %bitcast.28), calls=%async_computation.8 | async-start | bytes 262144 | tf_op jit(solution)/shard_map/all_to_all | solution.py:140
  172.8 22.4 %reduce-scatter.8.cloned.1.call-done = f32[512,128]{1,0:T(8,128)} async-done(((f32[2048,128]{1,0:T(8,128)}), f32[512,128]{1,0:T(8,128)}) %reduce-scatter.8.cloned.1.call-update) | async-done | bytes 262160 | tf_op jit(solution)/shard_map/reduce_scatter | solution.py:131
  195.2 1.9 fusion.34
  197.1 3.6 %all-to-all-start.8 = ((bf16[8,64,128]{2,1,0:T(8,128)(2,1)}), bf16[8,64,128]{2,1,0:T(8,128)(2,1)S(1)}, u32[]{:S(2)}, u32[]{:S(2)}) async-start(bf16[8,64,128]{2,1,0:T(8,128)(2,1)} %bitcast.31), calls=%async_computation.10 | async-start | bytes 262144 | tf_op jit(solution)/shard_map/all_to_all | solution.py:141
  201.4 4.8 %all-to-all-done.8 = bf16[8,64,128]{2,1,0:T(8,128)(2,1)S(1)} async-done(((bf16[8,64,128]{2,1,0:T(8,128)(2,1)}), bf16[8,64,128]{2,1,0:T(8,128)(2,1)S(1)}, u32[]{:S(2)}, u32[]{:S(2)}) %all-to-all-start.8) | async-done | bytes 131104 | tf_op jit(solution)/shard_map/all_to_all | solution.py:141
  (118 shorter events, 42.9 us)
Async XLA Ops:
  7.2 37.8 %copy-start.20 = (f32[512,1]{0,1:T(1,128)S(1)}, f32[512,1]{0,1:T(1,128)}, u32[]{:S(2)}) copy-start(f32[512,1]{0,1:T(1,128)} %param.25) | copy-start | bytes 6148
  7.2 37.8 %copy-start.16 = (bf16[512,128]{1,0:T(8,128)(2,1)S(1)}, bf16[512,128]{1,0:T(8,128)(2,1)}, u32[]{:S(2)}) copy-start(bf16[512,128]{1,0:T(8,128)(2,1)} %param.20) | copy-start | bytes 393220
  7.2 28.9 %copy-start.19 = (bf16[64,1024]{1,0:T(8,128)(2,1)S(1)}, bf16[64,1024]{1,0:T(8,128)(2,1)}, u32[]{:S(2)}) copy-start(bf16[64,1024]{1,0:T(8,128)(2,1)} %param.17) | copy-start | bytes 393220
  7.2 24.7 %all-to-all-start.1 = ((f32[64,8,1]{0,2,1:T(1,128)}), f32[64,8,1]{0,2,1:T(1,128)S(1)}, u32[]{:S(2)}, u32[]{:S(2)}) async-start(f32[64,8,1]{0,2,1:T(1,128)} %bitcast.179), calls=%async_computation.1 | async-start | bytes 8192 | tf_op jit(solution)/shard_map/all_to_all | solution.py:68
  23.4 30.4 %copy-start.11 = (bf16[512,128]{1,0:T(8,128)(2,1)S(1)}, bf16[512,128]{1,0:T(8,128)(2,1)}, u32[]{:S(2)}) copy-start(bf16[512,128]{1,0:T(8,128)(2,1)} %param.24) | copy-start | bytes 393220
  31.9 9.7 %all-to-all-start.4 = ((bf16[8,64,128]{2,1,0:T(8,128)(2,1)}), bf16[8,64,128]{2,1,0:T(8,128)(2,1)S(1)}, u32[]{:S(2)}, u32[]{:S(2)}) async-start(bf16[8,64,128]{2,1,0:T(8,128)(2,1)} %constant_dynamic-update-slice_fusion), calls=%async_computation.4 | async-start | bytes 262144 | tf_op jit(solution)/shard_map/all_to_all | solution.py:14
  41.6 8.8 %all-to-all-start.5 = ((bf16[64,8,128]{2,0,1:T(8,128)(2,1)}), bf16[64,8,128]{2,0,1:T(8,128)(2,1)S(1)}, u32[]{:S(2)}, u32[]{:S(2)}) async-start(bf16[64,8,128]{2,0,1:T(8,128)(2,1)} %copy_bitcast_fusion.3), calls=%async_computation.5 | async-start | bytes 262144 | tf_op jit(solution)/shard_map/all_to_all | solution.py:64
  45.3 22.7 %copy-start.4 = (f32[512,512]{0,1:T(8,128)}, f32[512,512]{0,1:T(8,128)S(1)}, u32[]{:S(2)}) copy-start(f32[512,512]{0,1:T(8,128)S(1)} %fusion.24) | copy-start | bytes 3145732
  50.4 8.8 %all-to-all-start.2 = ((bf16[64,8,128]{2,0,1:T(8,128)(2,1)}), bf16[64,8,128]{2,0,1:T(8,128)(2,1)S(1)}, u32[]{:S(2)}, u32[]{:S(2)}) async-start(bf16[64,8,128]{2,0,1:T(8,128)(2,1)} %copy_bitcast_fusion.5), calls=%async_computation.2 | async-start | bytes 262144 | tf_op jit(solution)/shard_map/all_to_all | solution.py:65
  54.9 22.3 %copy-start.18 = (bf16[512,128]{1,0:T(8,128)(2,1)S(1)}, bf16[512,128]{1,0:T(8,128)(2,1)}, u32[]{:S(2)}) copy-start(bf16[512,128]{1,0:T(8,128)(2,1)} %param.22) | copy-start | bytes 393220
  59.2 8.8 %all-to-all-start.3 = ((bf16[64,8,128]{2,0,1:T(8,128)(2,1)}), bf16[64,8,128]{2,0,1:T(8,128)(2,1)S(1)}, u32[]{:S(2)}, u32[]{:S(2)}) async-start(bf16[64,8,128]{2,0,1:T(8,128)(2,1)} %copy_bitcast_fusion.4), calls=%async_computation.3 | async-start | bytes 262144 | tf_op jit(solution)/shard_map/all_to_all | solution.py:66
  68.0 8.8 %all-to-all-start = ((bf16[64,8,128]{2,0,1:T(8,128)(2,1)}), bf16[64,8,128]{2,0,1:T(8,128)(2,1)S(1)}, u32[]{:S(2)}, u32[]{:S(2)}) async-start(bf16[64,8,128]{2,0,1:T(8,128)(2,1)} %copy_bitcast_fusion.6), calls=%async_computation | async-start | bytes 262144 | tf_op jit(solution)/shard_map/all_to_all | solution.py:62
  71.4 69.4 %reduce-scatter.10.cloned.1.call-start = ((), (), s32[]{:S(2)}) async-start(), calls=%async_computation.16 | async-start | bytes 327680 | tf_op jit(solution)/shard_map/reduce_scatter | solution.py:144
  72.1 70.2 %reduce-scatter.12.cloned.1.call-start = ((), (), s32[]{:S(2)}) async-start(), calls=%async_computation.17 | async-start | bytes 327680 | tf_op jit(solution)/shard_map/reduce_scatter | solution.py:145
  77.5 38.8 %copy-start.9 = (bf16[512,512]{1,0:T(8,128)(2,1)}, bf16[512,512]{1,0:T(8,128)(2,1)S(1)}, u32[]{:S(2)}) copy-start(bf16[512,512]{1,0:T(8,128)(2,1)S(1)} %fusion.27) | copy-start | bytes 1572868
  98.7 45.1 %reduce-scatter.14.cloned.1.call-start = ((), (), s32[]{:S(2)}) async-start(), calls=%async_computation.18 | async-start | bytes 327680 | tf_op jit(solution)/shard_map/reduce_scatter | solution.py:148
  117.2 50.0 %reduce-scatter.6.cloned.1.call-start = ((), (), s32[]{:S(2)}) async-start(), calls=%async_computation.14 | async-start | bytes 1310720 | tf_op jit(solution)/shard_map/reduce_scatter | solution.py:130
  130.9 36.3 %copy-start.8 = (bf16[512,512]{0,1:T(8,128)(2,1)S(1)}, bf16[512,512]{0,1:T(8,128)(2,1)}, u32[]{:S(2)}) copy-start(bf16[512,512]{0,1:T(8,128)(2,1)} %copy-done.7) | copy-start | bytes 1572868
  130.9 36.3 %copy-start.17 = (bf16[512,128]{1,0:T(8,128)(2,1)S(1)}, bf16[512,128]{1,0:T(8,128)(2,1)}, u32[]{:S(2)}) copy-start(bf16[512,128]{1,0:T(8,128)(2,1)} %param.20) | copy-start | bytes 393220
  130.9 64.3 %reduce-scatter.8.cloned.1.call-start = ((), (), s32[]{:S(2)}) async-start(), calls=%async_computation.15 | async-start | bytes 1310720 | tf_op jit(solution)/shard_map/reduce_scatter | solution.py:131
  130.9 64.2 %copy-start.5 = (f32[512,512]{0,1:T(8,128)S(1)}, f32[512,512]{0,1:T(8,128)}, u32[]{:S(2)}) copy-start(f32[512,512]{0,1:T(8,128)} %copy-done.4) | copy-start | bytes 3145732
  131.0 64.2 %copy-start.12 = (bf16[512,128]{1,0:T(8,128)(2,1)S(1)}, bf16[512,128]{1,0:T(8,128)(2,1)}, u32[]{:S(2)}) copy-start(bf16[512,128]{1,0:T(8,128)(2,1)} %param.24) | copy-start | bytes 393220
  169.1 28.0 %all-to-all-start.7 = ((bf16[8,64,128]{2,1,0:T(8,128)(2,1)}), bf16[8,64,128]{2,1,0:T(8,128)(2,1)S(1)}, u32[]{:S(2)}, u32[]{:S(2)}) async-start(bf16[8,64,128]{2,1,0:T(8,128)(2,1)} %bitcast.28), calls=%async_computation.8 | async-start | bytes 262144 | tf_op jit(solution)/shard_map/all_to_all | solution.py:140
  197.1 9.1 %all-to-all-start.8 = ((bf16[8,64,128]{2,1,0:T(8,128)(2,1)}), bf16[8,64,128]{2,1,0:T(8,128)(2,1)S(1)}, u32[]{:S(2)}, u32[]{:S(2)}) async-start(bf16[8,64,128]{2,1,0:T(8,128)(2,1)} %bitcast.31), calls=%async_computation.10 | async-start | bytes 262144 | tf_op jit(solution)/shard_map/all_to_all | solution.py:141
  (15 other events, 49.1 us)
Sparse Core Ops, SparseCore 0:
  74.5 23.0 reduce-scatter.9
  99.8 19.1 reduce-scatter.11
  121.3 18.1 reduce-scatter.13
  141.7 25.4 reduce-scatter.5
  169.3 25.7 reduce-scatter.7
